TPU v7x, 32 devices: a whole 2x2x4 slice. The times are simulated.
32 devices in a mesh: group: 2 (over y), tensor: 4 (over z), dp: 4 (over x, core).
Axes of the slice: x: 2, y: 2, z: 4, core: 2. Of those that a mesh axis runs over, the one named last changes fastest.
Arguments:
- teacher_input: bfloat16 [16, 257, 6144], P(('group', 'dp')), parts along dimension 0, may hold values from -1000 to 1000
- teacher_gain: float32 [6144], replicated, may hold values from 0.5 to 2
- teacher_weight: bfloat16 [6144, 2, 6144], P('dp', None, 'tensor'), may hold values from -30 to 30
- head_counts: int32 [48, 16], replicated, may hold values from 0 to 3
- assignment: int32 [16], P(('group', 'dp')), parts along dimension 0, may hold values from 0 to 7, each once
- student_input: bfloat16 [16, 257, 1024], P(('group', 'dp')), parts along dimension 0, may hold values from -1000 to 1000
- student_gain: float32 [1024], replicated, may hold values from 0.5 to 2
- student_bias: float32 [1024], replicated, may hold values from -3 to 3
- student_weight: bfloat16 [1024, 2048], P(None, 'tensor'), may hold values from -30 to 30
Outputs:
- weight_grad: float32 [2048, 2048], P('group', 'tensor'), parts along dimension 0
There are 2 independent parts, one for each index of `group`. A program takes and returns all parts, laid end to end along the dimension named above; an argument that names none is the same for every part. Nothing has to cross between parts.
Inputs may be any that keep to these rules, and one draw needn't show every extreme that they name: `assignment`: every image index of the group appears exactly once.
All inputs are finite; a program needn't handle non-finite values.
Results may differ from a plain program's by a relative error of at most 0.013.
The roundings to bfloat16 on the way count: a program that leaves them out, or rounds other values in their place, can miss the bound.
Values may be sent and summed in bfloat16 or wider, within the bound.
A program may use at most 192 MiB of HBM per device.

v0:
```python
import jax
import jax.numpy as jnp
from jax import lax
from jax.sharding import PartitionSpec as P

HD_T = 128
D_S = 1024
HD_S = 64
QROWS = 128
DIVISOR = 72


def layer_norm(values, gain, shift):
    wide = values.astype(jnp.float32)
    center = wide - jnp.mean(wide, axis=-1, keepdims=True)
    spread = jnp.mean(center * center, axis=-1, keepdims=True)
    return center * lax.rsqrt(spread + 1e-06) * gain + shift


def on_device(
    teacher_input,
    teacher_gain,
    teacher_weight,
    head_counts,
    assignment,
    student_input,
    student_gain,
    student_bias,
    student_weight,
):
    images = teacher_input.shape[0]
    tokens = teacher_input.shape[1]
    width_t = teacher_input.shape[2]
    teacher_cols = teacher_weight.shape[2]
    heads_here = teacher_cols // HD_T
    student_heads = student_weight.shape[1] // (2 * HD_S)
    tensor_place = lax.axis_index("tensor")
    teacher_normed = layer_norm(teacher_input, teacher_gain, 0.0).astype(jnp.bfloat16)
    normed_query = teacher_normed[:, :QROWS].reshape(images * QROWS, width_t)
    normed_keys = teacher_normed.reshape(images * tokens, width_t)
    piece = lax.all_gather(teacher_weight, "dp", axis=0, tiled=True)
    new_query = jnp.dot(normed_query, piece[:, 0, :], preferred_element_type=jnp.float32)
    new_keys = jnp.dot(normed_keys, piece[:, 1, :], preferred_element_type=jnp.float32)
    teacher_query = (
        (new_query * HD_T ** (-0.5)).astype(jnp.bfloat16).reshape(images, QROWS, heads_here, HD_T)
    )
    teacher_keys = new_keys.astype(jnp.bfloat16).reshape(images, tokens, heads_here, HD_T)
    teacher_scores = jnp.einsum(
        "bqhd,bkhd->bhqk", teacher_query, teacher_keys, preferred_element_type=jnp.float32
    )
    teacher_maps = jax.nn.softmax(teacher_scores, axis=-1).astype(jnp.bfloat16)
    own_counts = lax.dynamic_slice_in_dim(
        head_counts, tensor_place * heads_here, heads_here, 0
    ).astype(jnp.bfloat16)
    folded = lax.psum_scatter(
        (
            jnp.einsum(
                "bgqk,gs->sbqk", teacher_maps, own_counts, preferred_element_type=jnp.float32
            )
            / DIVISOR
        ).astype(jnp.bfloat16),
        "tensor",
        scatter_dimension=0,
        tiled=True,
    )
    piece = lax.all_gather(folded, "dp", axis=1, tiled=True)
    width_piece = piece.shape[1]
    positions = jnp.arange(width_piece, dtype=jnp.int32)
    picker = (assignment[:, None] == positions[None, :]).astype(jnp.bfloat16)
    target = jnp.einsum("ji,hiqk->hjqk", picker, piece, preferred_element_type=jnp.float32).astype(
        jnp.bfloat16
    )
    student_normed = layer_norm(student_input, student_gain, student_bias).astype(jnp.bfloat16)
    normed_front = student_normed[:, :QROWS]
    packed = student_weight.reshape(D_S, student_heads, 2, HD_S)
    weight_query = packed[:, :, 0, :].reshape(D_S, student_heads * HD_S)
    weight_key = packed[:, :, 1, :].reshape(D_S, student_heads * HD_S)
    student_query = (
        jnp.einsum("btd,dc->btc", normed_front, weight_query, preferred_element_type=jnp.float32)
        * HD_S ** (-0.5)
    ).astype(jnp.bfloat16)
    student_keys = jnp.einsum(
        "btd,dc->btc", student_normed, weight_key, preferred_element_type=jnp.float32
    ).astype(jnp.bfloat16)
    split_query = student_query.reshape(images, QROWS, student_heads, HD_S)
    split_keys = student_keys.reshape(images, tokens, student_heads, HD_S)
    probs = jax.nn.softmax(
        jnp.einsum("bqhd,bkhd->hbqk", split_query, split_keys, preferred_element_type=jnp.float32),
        axis=-1,
    )
    target_wide = target.astype(jnp.float32)
    score_grad = (probs * jnp.sum(target_wide, axis=-1, keepdims=True) - target_wide).astype(
        jnp.bfloat16
    )
    query_grad = (
        jnp.einsum("hbqk,bkhd->bqhd", score_grad, split_keys, preferred_element_type=jnp.float32)
        * HD_S ** (-0.5)
    ).astype(jnp.bfloat16)
    key_grad = jnp.einsum(
        "hbqk,bqhd->bkhd", score_grad, split_query, preferred_element_type=jnp.float32
    ).astype(jnp.bfloat16)
    grad_query = jnp.einsum(
        "fkm,fkp->mp",
        normed_front,
        query_grad.reshape(images, QROWS, student_heads * HD_S),
        preferred_element_type=jnp.float32,
    )
    grad_key = jnp.einsum(
        "oip,ois->ps",
        student_normed,
        key_grad.reshape(images, tokens, student_heads * HD_S),
        preferred_element_type=jnp.float32,
    )
    local_grad = jnp.stack(
        [grad_query.reshape(D_S, student_heads, HD_S), grad_key.reshape(D_S, student_heads, HD_S)],
        axis=2,
    )
    local_grad = local_grad.reshape(D_S, student_heads * 2 * HD_S)
    return lax.psum(local_grad.astype(jnp.bfloat16), "dp").astype(jnp.float32)


def solution(mesh):
    placed = (
        P(("group", "dp"), None, None),
        P(),
        P("dp", None, "tensor"),
        P(),
        P(("group", "dp")),
        P(("group", "dp"), None, None),
        P(),
        P(),
        P(None, "tensor"),
    )
    return jax.shard_map(
        on_device, mesh=mesh, in_specs=placed, out_specs=P("group", "tensor"), check_vma=False
    )
```

profile of v0, /device:TPU:0, one launch (start us, length us, event | category | flops | bytes accessed | tf_op | source)
XLA Modules:
  0.0 448.8 jit_solution(8952922629155033750)
XLA Ops:
  6.5 8.8 %copy.104 = bf16[1536,2,1536]{2,0,1:T(8,128)(2,1)} copy(bf16[1536,2,1536]{2,1,0:T(2,128)(2,1)} %param.11) | data formatting | bytes 18874368 | tf_op args[2]
  15.4 6.3 %convert_reduce_fusion = f32[2,257]{1,0:T(2,128)S(1)} fusion(bf16[2,257,6144]{2,0,1:T(2,128)(2,1)} %param.9), kind=kLoop, calls=%fused_computation.6 | loop fusion | flops 6315518 | bytes 6318088 | tf_op jit(solution)/shard_map/reduce_sum | solution.py:15
  21.7 3.5 fusion.5
  25.2 4.1 fusion.7
  29.4 4.6 %copy-done.1 = bf16[2,257,6144]{2,1,0:T(8,128)(2,1)} copy-done((bf16[2,257,6144]{2,1,0:T(8,128)(2,1)}, bf16[2,257,6144]{2,1,0:T(8,128)(2,1)S(1)}, u32[]{:S(2)}) %copy-start.1) | copy-done | bytes 6316056
  34.0 9.8 %reshape.81 = bf16[514,6144]{1,0:T(8,128)(2,1)} reshape(bf16[2,257,6144]{2,1,0:T(8,128)(2,1)} %copy-done.1) | data formatting | bytes 12632064 | tf_op jit(solution)/shard_map/reshape | solution.py:40
  43.7 202.4 %all-gather.3.cloned.1.call-done = bf16[6144,2,1536]{2,0,1:T(8,128)(2,1)} async-done(((bf16[1536,2,1536]{2,0,1:T(8,128)(2,1)}), bf16[6144,2,1536]{2,0,1:T(8,128)(2,1)}) %all-gather.3.cloned.1.call-update) | async-done | bytes 37748752 | tf_op jit(solution)/shard_map/all_gather | solution.py:41
  246.1 10.2 %fusion.10 = bf16[256,1536]{1,0:T(8,128)(2,1)} fusion(bf16[256,6144]{1,0:T(8,128)(2,1)S(1)} %bitcast.99, bf16[6144,2,1536]{2,0,1:T(8,128)(2,1)} %all-gather.3.cloned.1.call-done), kind=kOutput, calls=%fused_computation.19 | convolution fusion | flops 4832624640 | bytes 22806528 | tf_op jit(solution)/shard_map/dot_general | solution.py:42
  256.3 2.4 reshape.95
  258.6 16.2 %fusion.8 = bf16[514,1536]{1,0:T(8,128)(2,1)S(1)} fusion(bf16[514,6144]{1,0:T(8,128)(2,1)} %reshape.81, bf16[6144,2,1536]{2,0,1:T(8,128)(2,1)} %all-gather.3.cloned.1.call-done), kind=kOutput, calls=%fused_computation.15 | convolution fusion | flops 9702214656 | bytes 26843136 | tf_op jit(solution)/shard_map/dot_general | solution.py:43
  274.8 2.4 reshape.82
  277.2 3.1 fusion.61
  281.8 2.9 copy.109
  286.1 85.7 %all-reduce.6.cloned.1.call-done = bf16[16,2,128,257]{2,1,3,0:T(2,128)(2,1)} async-done(((bf16[16,2,128,257]{2,1,3,0:T(2,128)(2,1)}), bf16[16,2,128,257]{2,1,3,0:T(2,128)(2,1)}) %all-reduce.6.cloned.1.call-update) | async-done | bytes 2105360
  371.8 1.4 constant_dynamic-slice_fusion
  373.2 1.0 copy.110
  377.6 1.0 copy-done.3
  380.1 16.0 %all-gather.5.cloned.1.call-done = bf16[4,8,128,257]{2,0,3,1:T(4,128)(2,1)} async-done(((bf16[4,2,128,257]{2,0,3,1:T(4,128)(2,1)}), bf16[4,8,128,257]{2,0,3,1:T(4,128)(2,1)}) %all-gather.5.cloned.1.call-update) | async-done | bytes 2105360 | tf_op jit(solution)/shard_map/all_gather | solution.py:66
  396.1 2.4 fusion.17
  399.4 1.5 fusion.24
  401.0 1.0 fusion.25
  402.1 1.1 copy.117
  403.2 36.5 %all-reduce.4.cloned.1.call-done = bf16[1024,512]{0,1:T(8,128)(2,1)} async-done(((bf16[1024,512]{0,1:T(8,128)(2,1)}), bf16[1024,512]{0,1:T(8,128)(2,1)}) %all-reduce.4.cloned.1.call-update) | async-done | bytes 1048592 | tf_op jit(solution)/shard_map/psum | solution.py:119
  439.7 2.6 copy.118
  (52 shorter events, 8.1 us)
Async XLA Ops:
  6.5 239.5 %all-gather.3.cloned.1.call-start = ((), (), s32[]{:S(2)}) async-start(), calls=%async_computation | async-start | bytes 47185920 | tf_op jit(solution)/shard_map/all_gather | solution.py:41
  15.3 356.5 %all-reduce.6.cloned.1.call-start = ((), (), s32[]{:S(2)}) async-start(), calls=%async_computation.3 | async-start | bytes 4210688
  15.4 6.3 %copy-start = (bf16[2,257,6144]{2,0,1:T(2,128)(2,1)S(1)}, bf16[2,257,6144]{2,0,1:T(2,128)(2,1)}, u32[]{:S(2)}) copy-start(bf16[2,257,6144]{2,0,1:T(2,128)(2,1)} %param.9) | copy-start | bytes 18948100
  21.7 3.5 copy-start.5
  29.4 4.6 %copy-start.1 = (bf16[2,257,6144]{2,1,0:T(8,128)(2,1)}, bf16[2,257,6144]{2,1,0:T(8,128)(2,1)S(1)}, u32[]{:S(2)}) copy-start(bf16[2,257,6144]{2,1,0:T(8,128)(2,1)S(1)} %fusion.7) | copy-start | bytes 18948100
  34.0 212.1 %slice-start = ((bf16[2,257,6144]{2,1,0:T(8,128)(2,1)}), bf16[2,128,6144]{2,1,0:T(8,128)(2,1)S(1)}, s32[]{:S(2)}) async-start(bf16[2,257,6144]{2,1,0:T(8,128)(2,1)} %copy-done.1), calls=%async_computation.4 | async-start | bytes 6291456 | tf_op jit(solution)/shard_map/slice | solution.py:39
  280.4 0.7 copy-start.6
  281.8 3.0 copy-start.10
  284.8 89.5 %copy-start.4 = (bf16[1024,512]{1,0:T(8,128)(2,1)S(1)}, bf16[1024,512]{1,0:T(8,128)(2,1)}, u32[]{:S(2)}) copy-start(bf16[1024,512]{1,0:T(8,128)(2,1)} %param.17) | copy-start | bytes 3145732
  284.8 111.3 %all-gather.5.cloned.1.call-start = ((), (), s32[]{:S(2)}) async-start(), calls=%async_computation.1 | async-start | bytes 2631680 | tf_op jit(solution)/shard_map/all_gather | solution.py:66
  286.1 89.0 %copy-start.2 = (bf16[2,257,1024]{2,0,1:T(2,128)(2,1)S(1)}, bf16[2,257,1024]{2,0,1:T(2,128)(2,1)}, u32[]{:S(2)}) copy-start(bf16[2,257,1024]{2,0,1:T(2,128)(2,1)} %param.14) | copy-start | bytes 3158020
  374.3 65.4 %all-reduce.4.cloned.1.call-start = ((), (), s32[]{:S(2)}) async-start(), calls=%async_computation.2 | async-start | bytes 2097152 | tf_op jit(solution)/shard_map/psum | solution.py:119
  375.1 0.9 copy-start.7
  375.1 0.9 copy-start.8
  377.6 1.0 copy-start.3
  378.6 17.5 %copy-start.9 = (s32[2]{0:T(128)S(1)}, s32[2]{0:T(128)}, u32[]{:S(2)}) copy-start(s32[2]{0:T(128)} %param.13) | copy-start | bytes 28
Sparse Core Ops, SparseCore 0:
  15.5 230.5 all-gather.2
  284.9 86.8 all-reduce.5
  374.4 21.6 all-gather.4
  403.3 36.2 all-reduce.3
where the time goes:
time: 449 us
  waiting for transfers between devices  341 us (76%)
  local copies, waits for them, and re-layouts  40.2 us (9%)
  matrix products  36.8 us (8%)
  other arithmetic  17.1 us (4%)
  between operations  14 us (3%)
    all_gather x1, waiting for transfers between devices, on_device(): piece = lax.all_gather(teacher_weight, 'dp', axis=0, tiled=True)  202 us
    unnamed x5, waiting for transfers between devices  85.8 us
    psum x1, waiting for transfers between devices, on_device(): return lax.psum(local_grad.astype(jnp.bfloat16), 'dp').astype(jnp.float32)  36.5 us
    unnamed x26, local copies, waits for them, and re-layouts  17.6 us
    dot_general x1, matrix products, on_device(): jnp.dot(normed_keys, piece[:, 1, :], preferred_element_type=jnp.float32)  16.2 us
    all_gather x1, waiting for transfers between devices, on_device(): piece = lax.all_gather(folded, 'dp', axis=1, tiled=True)  16 us
    dot_general x1, matrix products, on_device(): jnp.dot(normed_query, piece[:, 0, :], preferred_element_type=jnp.float32)  10.2 us
    reshape x1, local copies, waits for them, and re-layouts, on_device(): normed_keys = teacher_normed.reshape(images * tokens, width_t)  9.77 us
  transfers between devices with their start and end apart: 4, of which 4 were waited for; matrix products, arithmetic and copies ran while one was open for 6% of the time, Pallas kernels for 0%

commit v1 on v0

--- a/solution.py
+++ b/solution.py
@@ -8,6 +8,12 @@
 HD_S = 64
 QROWS = 128
 DIVISOR = 72
+
+
+def joined_along(tiles, dim):
+    shape = list(tiles.shape[1:])
+    shape[dim] *= tiles.shape[0]
+    return jnp.moveaxis(tiles, 0, dim).reshape(shape)
 
 
 def layer_norm(values, gain, shift):
@@ -38,7 +44,19 @@
     teacher_normed = layer_norm(teacher_input, teacher_gain, 0.0).astype(jnp.bfloat16)
     normed_query = teacher_normed[:, :QROWS].reshape(images * QROWS, width_t)
     normed_keys = teacher_normed.reshape(images * tokens, width_t)
-    piece = lax.all_gather(teacher_weight, "dp", axis=0, tiled=True)
+    size = lax.axis_size("dp")
+    pairs = [(i, (i + 1) % size) for i in range(size)]
+    back = [(b, a) for a, b in pairs]
+    lower, upper = ([], [])
+    for hop in range(size - 1):
+        if hop % 2 == 0:
+            lower.append(lax.ppermute(lower[-1] if lower else teacher_weight, "dp", pairs))
+        else:
+            upper.append(lax.ppermute(upper[-1] if upper else teacher_weight, "dp", back))
+    parts = jnp.stack([*lower[::-1], teacher_weight, *upper])
+    shift_2 = lax.axis_index("dp") - len(lower)
+    parts = parts[(jnp.arange(size) - shift_2) % size]
+    piece = joined_along(parts, 0)
     new_query = jnp.dot(normed_query, piece[:, 0, :], preferred_element_type=jnp.float32)
     new_keys = jnp.dot(normed_keys, piece[:, 1, :], preferred_element_type=jnp.float32)
     teacher_query = (

time: 449 us -> 980 us (2.18)
  other arithmetic: 17.1 us -> 296 us
  local copies, waits for them, and re-layouts: 40.2 us -> 201 us
  waiting for transfers between devices: 341 us -> 421 us
    ppermute x0 -> x3, waiting for transfers between devices: none -> 279 us  [the longest x2 279 us: on_device(): lax.ppermute(lower[-1] if lower else teacher_weight, 'dp', pairs)]
    unnamed x0 -> x1, other arithmetic: none -> 205 us
    all_gather x1 -> x0, waiting for transfers between devices: 202 us -> none  [on_device(): piece = lax.all_gather(teacher_weight, 'dp', axis=0, tiled=True)]
    gather x0 -> x33, local copies, waits for them, and re-layouts: none -> 124 us
    another operation x0 -> x1, other arithmetic: none -> 73.5 us  [on_device(): parts = jnp.stack([*lower[::-1], teacher_weight, *upper])]
    unnamed x26 -> x30, local copies, waits for them, and re-layouts: 17.6 us -> 57.2 us
    unnamed x5 -> x4, waiting for transfers between devices: 85.8 us -> 89.6 us
  transfers between devices with their start and end apart: 4 -> 6, of which waited for: 4 -> 5; matrix products, arithmetic and copies ran while one was open for 6% -> 3% of each run, Pallas kernels for 0% -> 0%
where the time goes in v1:
time: 980 us; the launch traced here: 974 us
  waiting for transfers between devices  421 us (43%)
  other arithmetic  296 us (30%)
  local copies, waits for them, and re-layouts  201 us (21%)
  matrix products  36.6 us (4%)
  between operations  14.3 us (1%)
    ppermute x2, waiting for transfers between devices, on_device(): lax.ppermute(lower[-1] if lower else teacher_weight, 'dp', pairs)  279 us
    unnamed x1, other arithmetic  205 us
    gather x32, local copies, waits for them, and re-layouts  93.3 us
    unnamed x4, waiting for transfers between devices  89.6 us
    another operation x1, other arithmetic, on_device(): parts = jnp.stack([*lower[::-1], teacher_weight, *upper])  73.5 us
    unnamed x30, local copies, waits for them, and re-layouts  57.2 us
    psum x1, waiting for transfers between devices, on_device(): return lax.psum(local_grad.astype(jnp.bfloat16), 'dp').astype(jnp.float32)  36.5 us
    gather x1, local copies, waits for them, and re-layouts, on_device(): parts = parts[(jnp.arange(size) - shift_2) % size]  30.2 us
  transfers between devices with their start and end apart: 6, of which 5 were waited for; matrix products, arithmetic and copies ran while one was open for 3% of the time, Pallas kernels for 0%

profile of v1, /device:TPU:0, one launch (start us, length us, event | category | flops | bytes accessed | tf_op | source)
XLA Modules:
  0.0 973.6 jit_solution(4974045684985609441)
XLA Ops:
  8.9 201.2 %collective-permute-done = bf16[1536,2,1536]{2,1,0:T(2,128)(2,1)} collective-permute-done((bf16[1536,2,1536]{2,1,0:T(2,128)(2,1)}, bf16[1536,2,1536]{2,1,0:T(2,128)(2,1)}, u32[]{:S(2)}, u32[]{:S(2)}) %collective-permute-start) | collective-permute-done | bytes 9437216 | tf_op jit(solution)/shard_map/ppermute | solution.py:53
  212.7 6.3 convert_reduce_fusion
  229.6 7.0 reshape.134
  236.7 77.9 %collective-permute-done.1 = bf16[1536,2,1536]{2,1,0:T(2,128)(2,1)} collective-permute-done((bf16[1536,2,1536]{2,1,0:T(2,128)(2,1)}, bf16[1536,2,1536]{2,1,0:T(2,128)(2,1)}, u32[]{:S(2)}, u32[]{:S(2)}) %collective-permute-start.1) | collective-permute-done | bytes 9437216 | tf_op jit(solution)/shard_map/ppermute | solution.py:53
  314.6 73.5 %pad_maximum_fusion = bf16[4,1536,2,1536]{3,2,1,0:T(2,128)(2,1)} fusion(bf16[1,1536,2,1536]{3,2,1,0:T(2,128)(2,1)} %bitcast.13, bf16[1,1536,2,1536]{3,2,1,0:T(2,128)(2,1)} %bitcast.119, bf16[1,1536,2,1536]{3,2,1,0:T(2,128)(2,1)} %bitcast.11, bf16[1,1536,2,1536]{3,2,1,0:T(2,128)(2,1)} %bitcast.10), kind=kLoop, calls=%fused_computation.9 | loop fusion | flops 56623104 | bytes 75497472 | tf_op jit(solution)/shard_map/stack | solution.py:56
  388.1 30.2 %fusion.61 = (bf16[4,384,2,1536]{3,2,1,0:T(2,128)(2,1)}, bf16[4,384,2,1536]{3,2,1,0:T(2,128)(2,1)}, bf16[4,384,2,1536]{3,2,1,0:T(2,128)(2,1)}, bf16[4,384,2,1536]{3,2,1,0:T(2,128)(2,1)}) fusion(bf16[4,1536,2,1536]{3,2,1,0:T(2,128)(2,1)} %pad_maximum_fusion), kind=kLoop, calls=%fused_computation.92 | loop fusion | bytes 75497472 | tf_op jit(solution)/shard_map/gather | solution.py:58
  418.3 6.1 broadcast.122.clone.3
  424.4 23.4 %while.4 = (s32[]{:T(128)}, bf16[4,384,2,1536]{3,2,1,0:T(2,128)(2,1)}, s32[4,1]{0,1:T(1,128)S(1)}, bf16[4,384,2,1536]{3,2,1,0:T(2,128)(2,1)}, s32[]{:T(128)}) while((s32[]{:T(128)}, bf16[4,384,2,1536]{3,2,1,0:T(2,128)(2,1)}, s32[4,1]{0,1:T(1,128)S(1)}, bf16[4,384,2,1536]{3,2,1,0:T(2,128)(2,1)}, s32[]{:T(128)}) %tuple.64), condition=%wide.while_cond, body=%wide.while_body.sunk | while | flops 2 | bytes 4719689 | solution.py:58
  430.9 5.3 dynamic-slice_dynamic-update-slice_fusion.8
  447.8 6.1 broadcast.122.clone.2
  454.0 23.3 %while.5 = (s32[]{:T(128)}, bf16[4,384,2,1536]{3,2,1,0:T(2,128)(2,1)}, s32[4,1]{0,1:T(1,128)S(1)}, bf16[4,384,2,1536]{3,2,1,0:T(2,128)(2,1)}, s32[]{:T(128)}) while((s32[]{:T(128)}, bf16[4,384,2,1536]{3,2,1,0:T(2,128)(2,1)}, s32[4,1]{0,1:T(1,128)S(1)}, bf16[4,384,2,1536]{3,2,1,0:T(2,128)(2,1)}, s32[]{:T(128)}) %tuple.73), condition=%wide.while_cond.1, body=%wide.while_body.1.sunk | while | flops 2 | bytes 4719689 | solution.py:58
  466.2 5.3 dynamic-slice_dynamic-update-slice_fusion.9
  477.3 6.1 broadcast.122.clone.1
  483.4 23.4 %while.6 = (s32[]{:T(128)}, bf16[4,384,2,1536]{3,2,1,0:T(2,128)(2,1)}, s32[4,1]{0,1:T(1,128)S(1)}, bf16[4,384,2,1536]{3,2,1,0:T(2,128)(2,1)}, s32[]{:T(128)}) while((s32[]{:T(128)}, bf16[4,384,2,1536]{3,2,1,0:T(2,128)(2,1)}, s32[4,1]{0,1:T(1,128)S(1)}, bf16[4,384,2,1536]{3,2,1,0:T(2,128)(2,1)}, s32[]{:T(128)}) %tuple.74), condition=%wide.while_cond.2, body=%wide.while_body.2.sunk | while | flops 2 | bytes 4719689 | solution.py:58
  489.8 5.3 dynamic-slice_dynamic-update-slice_fusion.10
  506.8 6.1 broadcast.122.clone
  512.9 23.4 %while.7 = (s32[]{:T(128)}, bf16[4,384,2,1536]{3,2,1,0:T(2,128)(2,1)}, s32[4,1]{0,1:T(1,128)S(1)}, bf16[4,384,2,1536]{3,2,1,0:T(2,128)(2,1)}, s32[]{:T(128)}) while((s32[]{:T(128)}, bf16[4,384,2,1536]{3,2,1,0:T(2,128)(2,1)}, s32[4,1]{0,1:T(1,128)S(1)}, bf16[4,384,2,1536]{3,2,1,0:T(2,128)(2,1)}, s32[]{:T(128)}) %tuple.75), condition=%wide.while_cond.3, body=%wide.while_body.3.sunk | while | flops 2 | bytes 4719689 | solution.py:58
  536.3 204.7 %pad_maximum_fusion.1 = bf16[4,1536,2,1536]{3,2,1,0:T(2,128)(2,1)} fusion(bf16[4,384,2,1536]{3,2,1,0:T(2,128)(2,1)} %get-tuple-element.36, bf16[4,384,2,1536]{3,2,1,0:T(2,128)(2,1)} %get-tuple-element.28, bf16[4,384,2,1536]{3,2,1,0:T(2,128)(2,1)} %get-tuple-element.20, bf16[4,384,2,1536]{3,2,1,0:T(2,128)(2,1)} %get-tuple-element.12), kind=kLoop, calls=%fused_computation.10 | loop fusion | flops 56623104 | bytes 75497472
  741.0 26.0 %copy.104 = bf16[4,1536,2,1536]{3,1,0,2:T(8,128)(2,1)} copy(bf16[4,1536,2,1536]{3,2,1,0:T(2,128)(2,1)} %pad_maximum_fusion.1) | data formatting | bytes 75497472
  767.0 10.2 %fusion.10 = bf16[256,1536]{1,0:T(8,128)(2,1)} fusion(bf16[256,6144]{1,0:T(8,128)(2,1)S(1)} %bitcast.116, bf16[6144,2,1536]{2,0,1:T(8,128)(2,1)} %bitcast.117), kind=kOutput, calls=%fused_computation.29 | convolution fusion | flops 4832624640 | bytes 22806528 | tf_op jit(solution)/shard_map/dot_general | solution.py:60
  779.6 16.0 %fusion.8 = bf16[514,1536]{1,0:T(8,128)(2,1)S(1)} fusion(bf16[514,6144]{1,0:T(8,128)(2,1)} %reshape.134, bf16[6144,2,1536]{2,0,1:T(8,128)(2,1)} %bitcast.118), kind=kOutput, calls=%fused_computation.25 | convolution fusion | flops 9702214656 | bytes 26843136 | tf_op jit(solution)/shard_map/dot_general | solution.py:61
  806.9 89.6 %all-reduce.6.cloned.1.call-done = bf16[16,2,128,257]{2,1,3,0:T(2,128)(2,1)} async-done(((bf16[16,2,128,257]{2,1,3,0:T(2,128)(2,1)}), bf16[16,2,128,257]{2,1,3,0:T(2,128)(2,1)}) %all-reduce.6.cloned.1.call-update) | async-done | bytes 2105360
  904.5 16.2 %all-gather.2.cloned.1.call-done = bf16[4,8,128,257]{2,0,3,1:T(4,128)(2,1)} async-done(((bf16[4,2,128,257]{2,0,3,1:T(4,128)(2,1)}), bf16[4,8,128,257]{2,0,3,1:T(4,128)(2,1)}) %all-gather.2.cloned.1.call-update) | async-done | bytes 2105360 | tf_op jit(solution)/shard_map/all_gather | solution.py:84
  927.8 36.5 %all-reduce.4.cloned.1.call-done = bf16[1024,512]{0,1:T(8,128)(2,1)} async-done(((bf16[1024,512]{0,1:T(8,128)(2,1)}), bf16[1024,512]{0,1:T(8,128)(2,1)}) %all-reduce.4.cloned.1.call-update) | async-done | bytes 1048592 | tf_op jit(solution)/shard_map/psum | solution.py:137
  (99 shorter events, 123.4 us)
Async XLA Ops:
  6.5 889.9 %all-reduce.6.cloned.1.call-start = ((), (), s32[]{:S(2)}) async-start(), calls=%async_computation.2 | async-start | bytes 4210688
  6.5 203.6 %collective-permute-start = (bf16[1536,2,1536]{2,1,0:T(2,128)(2,1)}, bf16[1536,2,1536]{2,1,0:T(2,128)(2,1)}, u32[]{:S(2)}, u32[]{:S(2)}) collective-permute-start(bf16[1536,2,1536]{2,1,0:T(2,128)(2,1)} %param.11), channel_id=1, source_target_pairs={{0,1},{1,2},{2,3},{3,0},{4,5},{5,6},{6,7},{7,4},{8,9},{9,10},{10,1... | collective-permute-start | bytes 28311560 | tf_op jit(solution)/shard_map/ppermute | solution.py:53
  7.0 229.6 %collective-permute-start.2 = (bf16[1536,2,1536]{2,1,0:T(2,128)(2,1)}, bf16[1536,2,1536]{2,1,0:T(2,128)(2,1)}, u32[]{:S(2)}, u32[]{:S(2)}) collective-permute-start(bf16[1536,2,1536]{2,1,0:T(2,128)(2,1)} %param.11), channel_id=1, source_target_pairs={{1,0},{2,1},{3,2},{0,3},{5,4},{6,5},{7,6},{4,7},{9,8},{10,9},{11,1... | collective-permute-start | bytes 28311560 | tf_op jit(solution)/shard_map/ppermute | solution.py:55
  210.1 104.4 %collective-permute-start.1 = (bf16[1536,2,1536]{2,1,0:T(2,128)(2,1)}, bf16[1536,2,1536]{2,1,0:T(2,128)(2,1)}, u32[]{:S(2)}, u32[]{:S(2)}) collective-permute-start(bf16[1536,2,1536]{2,1,0:T(2,128)(2,1)} %collective-permute-done), channel_id=1, source_target_pairs={{0,1},{1,2},{2,3},{3,0},{4,5},{5,6},{6,7},{7,4},{8,9},{9,10},{10,1... | collective-permute-start | bytes 28311560 | tf_op jit(solution)/shard_map/ppermute | solution.py:53
  212.7 6.3 copy-start
  219.0 3.5 copy-start.5
  226.9 2.7 copy-start.1
  741.0 26.0 %slice-start = ((bf16[2,257,6144]{2,1,0:T(8,128)(2,1)}), bf16[2,128,6144]{2,1,0:T(8,128)(2,1)S(1)}, s32[]{:S(2)}) async-start(bf16[2,257,6144]{2,1,0:T(8,128)(2,1)} %copy-done.1), calls=%async_computation.3 | async-start | bytes 6291456 | tf_op jit(solution)/shard_map/slice | solution.py:45
  801.2 0.7 copy-start.6
  802.6 3.0 copy-start.10
  805.6 93.4 %copy-start.4 = (bf16[1024,512]{1,0:T(8,128)(2,1)S(1)}, bf16[1024,512]{1,0:T(8,128)(2,1)}, u32[]{:S(2)}) copy-start(bf16[1024,512]{1,0:T(8,128)(2,1)} %param.17) | copy-start | bytes 3145732
  805.6 94.0 %copy-start.2 = (bf16[2,257,1024]{2,0,1:T(2,128)(2,1)S(1)}, bf16[2,257,1024]{2,0,1:T(2,128)(2,1)}, u32[]{:S(2)}) copy-start(bf16[2,257,1024]{2,0,1:T(2,128)(2,1)} %param.14) | copy-start | bytes 3158020
  805.6 115.1 %all-gather.2.cloned.1.call-start = ((), (), s32[]{:S(2)}) async-start(), calls=%async_computation | async-start | bytes 2631680 | tf_op jit(solution)/shard_map/all_gather | solution.py:84
  898.9 1.5 copy-start.7
  898.9 1.5 copy-start.8
  898.9 65.4 %all-reduce.4.cloned.1.call-start = ((), (), s32[]{:S(2)}) async-start(), calls=%async_computation.1 | async-start | bytes 2097152 | tf_op jit(solution)/shard_map/psum | solution.py:137
  900.9 1.0 copy-start.3
  902.4 18.3 %copy-start.9 = (s32[2]{0:T(128)S(1)}, s32[2]{0:T(128)}, u32[]{:S(2)}) copy-start(s32[2]{0:T(128)} %param.13) | copy-start | bytes 28
Sparse Core Ops, SparseCore 0:
  805.7 90.7 all-reduce.5
  899.0 21.6 all-gather.1
  928.0 36.2 all-reduce.3
